TPU v7x, 256 devices: a whole 4x4x8 slice. The times are simulated.
256 devices in a mesh: row: 16 (over z_lo, y), col: 16 (over z_hi, x, core).
Axes of the slice: x: 4, y: 4, z: 8 (z_hi: 2, z_lo: 4; z = z_hi * 4 + z_lo), core: 2. Of those that a mesh axis runs over, the one named last changes fastest.
Arguments:
- object_field: float32 [2, 2048, 2048], P(None, 'row', 'col'), may hold values from -5 to 5
- probe: float32 [2, 2, 256, 256], replicated, may hold values from -5 to 5
- amplitudes: float32 [16, 16, 2, 256, 256], P('row', 'col'), may hold values from 0.2 to 2.5
- offsets: int32 [16, 16, 2, 2], P('row', 'col'), may hold values from -128 to 0
Outputs:
- object_out: float32 [2, 2048, 2048], P(None, 'row', 'col')
- probe_out: float32 [2, 2, 256, 256], replicated
Inputs may be any that keep to these rules, and one draw needn't show every extreme that they name: `offsets`: each scan's 256 x 256 window starts at this offset from its own tile's anchor, so it reaches at most 128 pixels into neighbouring tiles.
All inputs are finite; a program needn't handle non-finite values.
Results may differ from a plain program's by a relative error of at most 0.0003.
Values sent between devices are 32-bit elements; how exact they have to be, the bound alone decides.
No kernel may reach another device: no remote copies, remote signals or barrier semaphores. Data moves between devices by JAX's collectives and lax.ppermute only.
A program may use at most 128 MiB of HBM per device.

v0:
```python
import math
import jax
import jax.numpy as jnp
from jax import lax
from jax.sharding import PartitionSpec as P

ITERS = 2
FLOOR = 0.5
OBJECT_STEP = 0.5
OBJECT_REG = 0.5
PROBE_STEP = 1.0
PROBE_REG = 1.0
HIGHEST = lax.Precision.HIGHEST


def padded_2(cells, sides, width):
    for axis, dim in sides:
        count = lax.axis_size(axis)
        ends = count - 1
        head = lax.slice_in_dim(cells, 0, width, axis=dim)
        tail = lax.slice_in_dim(cells, cells.shape[dim] - width, cells.shape[dim], axis=dim)
        cells = jnp.concatenate(
            [
                lax.ppermute(tail, axis, [(i, (i + 1) % count) for i in range(ends)]),
                cells,
                lax.ppermute(head, axis, [((i + 1) % count, i) for i in range(ends)]),
            ],
            axis=dim,
        )
    return cells


def tables(side):
    indices = lax.iota(jnp.int32, side)
    phases = indices[:, None] * indices[None, :] % side
    angles = phases.astype(jnp.float32) * (2.0 * math.pi / side)
    scaling = 1.0 / math.sqrt(side)
    return (jnp.cos(angles) * scaling, jnp.sin(angles) * scaling)


def last_axis(real_part, imag_part, cos_table, sin_table):
    product_one = jnp.matmul(real_part, cos_table, precision=HIGHEST)
    product_two = jnp.matmul(imag_part, sin_table, precision=HIGHEST)
    product_three = jnp.matmul(real_part + imag_part, cos_table + sin_table, precision=HIGHEST)
    return (product_one - product_two, product_three - product_one - product_two)


def first_axis(real_part, imag_part, cos_table, sin_table):
    product_one = jnp.einsum("jk,bkl->bjl", cos_table, real_part, precision=HIGHEST)
    product_two = jnp.einsum("jk,bkl->bjl", sin_table, imag_part, precision=HIGHEST)
    product_three = jnp.einsum(
        "jk,bkl->bjl", cos_table + sin_table, real_part + imag_part, precision=HIGHEST
    )
    return (product_one - product_two, product_three - product_one - product_two)


def transform(real_part, imag_part, cos_table, sin_table):
    real_part, imag_part = last_axis(real_part, imag_part, cos_table, sin_table)
    return first_axis(real_part, imag_part, cos_table, sin_table)


def fold_axis(extended, axis_number, tile_side, half_width):
    own_part = lax.slice_in_dim(
        extended, 2 * half_width, 2 * half_width + tile_side, axis=axis_number
    )
    low_rim = lax.slice_in_dim(extended, 0, half_width, axis=axis_number)
    high_rim = lax.slice_in_dim(
        extended, tile_side + 3 * half_width, tile_side + 4 * half_width, axis=axis_number
    )
    low_widths = [(0, 0)] * extended.ndim
    high_widths = [(0, 0)] * extended.ndim
    low_widths[axis_number] = (0, tile_side - half_width)
    high_widths[axis_number] = (tile_side - half_width, 0)
    return own_part + low_rim + high_rim


def cut_windows(padded, starts, probe_side):
    zero_index = jnp.zeros((), jnp.int32)

    def cut_one(corner):
        return lax.dynamic_slice(
            padded, (zero_index, corner[0], corner[1]), (padded.shape[0], probe_side, probe_side)
        )

    return jax.vmap(cut_one)(starts)


def local(object_field, probe, amplitudes, offsets):
    tile_side = object_field.shape[1]
    mode_count = probe.shape[1]
    probe_side = probe.shape[2]
    half_width = probe_side // 2
    starts = offsets[0, 0] + half_width
    measured = amplitudes[0, 0]
    scan_count = starts.shape[0]
    zero_index = jnp.zeros((), jnp.int32)
    cos_table, sin_table = tables(probe_side)
    padded = padded_2(object_field, (("row", 1), ("col", 2)), half_width)
    for iteration in range(ITERS):
        windows = cut_windows(padded, starts, probe_side)
        win_real = windows[:, 0][:, None]
        win_imag = windows[:, 1][:, None]
        probe_real = probe[0][None]
        probe_imag = probe[1][None]
        exit_real = (probe_real * win_real - probe_imag * win_imag).reshape(
            -1, probe_side, probe_side
        )
        exit_imag = (probe_real * win_imag + probe_imag * win_real).reshape(
            -1, probe_side, probe_side
        )
        far_real, far_imag = transform(exit_real, exit_imag, cos_table, -sin_table)
        far_real = far_real.reshape(scan_count, mode_count, probe_side, probe_side)
        far_imag = far_imag.reshape(scan_count, mode_count, probe_side, probe_side)
        intensity = jnp.sum(far_real * far_real + far_imag * far_imag, axis=1)
        factor = (measured / jnp.maximum(jnp.sqrt(intensity), FLOOR) - 1.0)[:, None]
        back_real, back_imag = transform(
            (far_real * factor).reshape(-1, probe_side, probe_side),
            (far_imag * factor).reshape(-1, probe_side, probe_side),
            cos_table,
            sin_table,
        )
        back_real = back_real.reshape(scan_count, mode_count, probe_side, probe_side)
        back_imag = back_imag.reshape(scan_count, mode_count, probe_side, probe_side)
        obj_real = jnp.sum(probe_real * back_real + probe_imag * back_imag, axis=1)
        obj_imag = jnp.sum(probe_real * back_imag - probe_imag * back_real, axis=1)
        probe_power = jnp.sum(probe[0] * probe[0] + probe[1] * probe[1], axis=0)
        grad_probe = jnp.stack(
            [
                jnp.sum(win_real * back_real + win_imag * back_imag, axis=0),
                jnp.sum(win_real * back_imag - win_imag * back_real, axis=0),
            ]
        )
        probe_weight = jnp.sum(
            windows[:, 0] * windows[:, 0] + windows[:, 1] * windows[:, 1], axis=0
        )
        channels = 3
        gradient = jnp.zeros(
            (channels, tile_side + 2 * half_width, tile_side + 2 * half_width), jnp.float32
        )
        for scan_index in range(scan_count):
            contrib = jnp.stack([obj_real[scan_index], obj_imag[scan_index], probe_power])
            corner = (zero_index, starts[scan_index, 0], starts[scan_index, 1])
            gradient = lax.dynamic_update_slice(
                gradient, lax.dynamic_slice(gradient, corner, contrib.shape) + contrib, corner
            )
        extended = padded_2(gradient, (("row", 1), ("col", 2)), half_width)
        totals = fold_axis(fold_axis(extended, 1, tile_side, half_width), 2, tile_side, half_width)
        summed_grad, summed_weight = lax.psum((grad_probe, probe_weight), ("row", "col"))
        new_probe = probe + PROBE_STEP * summed_grad / (summed_weight + PROBE_REG)
        object_field = object_field + OBJECT_STEP * totals[0:2] / (totals[2:3] + OBJECT_REG)
        if iteration + 1 < ITERS:
            padded = padded_2(object_field, (("row", 1), ("col", 2)), half_width)
        probe = new_probe
    return (object_field, probe)


def solution(mesh):
    return jax.shard_map(
        local,
        mesh=mesh,
        in_specs=(
            P(None, "row", "col"),
            P(),
            P("row", "col", None, None, None),
            P("row", "col", None, None),
        ),
        out_specs=(P(None, "row", "col"), P()),
        check_vma=False,
    )
```

profile of v0, /device:TPU:2, one launch (start us, length us, event | category | flops | bytes accessed | tf_op | source)
XLA Modules:
  0.0 828.7 jit_solution(15070879831426267204)
XLA Ops:
  7.2 3.6 collective-permute-start
  19.9 3.6 collective-permute-start.3
  36.4 4.3 while.2
  49.5 3.9 fusion.53
  72.7 13.8 %fusion.10 = f32[4,256,256]{2,1,0:T(8,128)S(1)} fusion(f32[4,256,256]{2,1,0:T(8,128)S(1)} %fusion.43, f32[4,256,256]{2,1,0:T(8,128)S(1)} %fusion.62, f32[4,256,256]{1,2,0:T(8,128)S(1)} %get-tuple-element.94, f32[4,256,256]{1,2,0:T(8,128)S(1)} %get-tuple-element.95), kind=kOutput, calls=%fused_computation.34 | convolution fusion | flops 807206912 | bytes 5242880 | tf_op jit(solution)/shard_map/dot_general | solution.py:44
  91.9 4.6 add_reduce_fusion.3
  98.3 10.7 %dynamic_update_slice.12 = f32[3,384,384]{1,2,0:T(8,128)S(1)} dynamic-update-slice(f32[3,384,384]{1,2,0:T(8,128)S(1)} %broadcast.83.clone, f32[3,256,256]{1,2,0:T(8,128)} %pad_maximum_fusion.5, s32[]{:T(128)} %constant.12.clone.1, s32[]{:T(128)S(6)} %select_n.86, s32[]{:T(128)S(6)} %select_n.87) | dynamic-update-slice | bytes 1572868 | tf_op jit(solution)/shard_map/dynamic_update_slice | solution.py:143
  111.0 11.3 %dynamic_update_slice.13 = f32[3,384,384]{1,2,0:T(8,128)S(1)} dynamic-update-slice(f32[3,384,384]{1,2,0:T(8,128)S(1)} %dynamic_update_slice.12, f32[3,256,256]{1,2,0:T(8,128)} %fusion.21, s32[]{:T(128)} %constant.12.clone.1, s32[]{:T(128)S(6)} %select_n.88, s32[]{:T(128)S(6)} %select_n.89) | dynamic-update-slice | bytes 1572868 | tf_op jit(solution)/shard_map/dynamic_update_slice | solution.py:143
  129.2 8.5 %collective-permute-done.4 = f32[3,128,384]{1,2,0:T(8,128)S(1)} collective-permute-done((f32[3,128,384]{1,2,0:T(8,128)S(1)}, f32[3,128,384]{1,2,0:T(8,128)S(1)}, u32[]{:S(2)}, u32[]{:S(2)}) %collective-permute-start.4) | collective-permute-done | bytes 589856 | tf_op jit(solution)/shard_map/ppermute | solution.py:24
  137.6 4.8 collective-permute-done.5
  145.9 3.6 collective-permute-start.7
  153.5 265.9 %all-reduce.7.cloned.1.call-done = (f32[2,2,256,256]{2,3,1,0:T(8,128)}, f32[256,256]{1,0:T(8,128)}) async-done(((f32[2,2,256,256]{2,3,1,0:T(8,128)}, f32[256,256]{1,0:T(8,128)}), (f32[2,2,256,256]{2,3,1,0:T(8,128)}, f32[256,256]{1,0:T(8,128)})) %all-reduce.7.cloned.1.call-update) | async-done | bytes 1310736 | tf_op jit(solution)/shard_map/psum | solution.py:148
  428.5 4.4 collective-permute-done.9
  434.8 3.6 collective-permute-start.11
  444.9 7.5 while.3
  458.6 3.9 fusion.50
  483.2 3.0 fusion.8
  491.6 4.5 add_reduce_fusion.1
  498.0 10.7 %dynamic_update_slice.14 = f32[3,384,384]{1,2,0:T(8,128)S(1)} dynamic-update-slice(f32[3,384,384]{1,2,0:T(8,128)S(1)} %broadcast.83, f32[3,256,256]{1,2,0:T(8,128)} %pad_maximum_fusion.7, s32[]{:T(128)} %constant.12.clone.1, s32[]{:T(128)S(6)} %select_n.86, s32[]{:T(128)S(6)} %select_n.87) | dynamic-update-slice | bytes 1572868 | tf_op jit(solution)/shard_map/dynamic_update_slice | solution.py:143
  510.8 11.6 %dynamic_update_slice.15 = f32[3,384,384]{1,2,0:T(8,128)S(1)} dynamic-update-slice(f32[3,384,384]{1,2,0:T(8,128)S(1)} %dynamic_update_slice.14, f32[3,256,256]{1,2,0:T(8,128)} %fusion.20, s32[]{:T(128)} %constant.12.clone.1, s32[]{:T(128)S(6)} %select_n.88, s32[]{:T(128)S(6)} %select_n.89) | dynamic-update-slice | bytes 1572868 | tf_op jit(solution)/shard_map/dynamic_update_slice | solution.py:143
  531.5 8.1 collective-permute-done.12
  539.6 4.2 collective-permute-done.13
  548.6 3.2 collective-permute-start.15
  551.8 258.8 %all-reduce.5.cloned.1.call-done = (f32[2,2,256,256]{2,3,1,0:T(8,128)}, f32[256,256]{1,0:T(8,128)}) async-done(((f32[2,2,256,256]{2,3,1,0:T(8,128)}, f32[256,256]{1,0:T(8,128)}), (f32[2,2,256,256]{2,3,1,0:T(8,128)}, f32[256,256]{1,0:T(8,128)})) %all-reduce.5.cloned.1.call-update) | async-done | bytes 1310736 | tf_op jit(solution)/shard_map/psum | solution.py:148
  (198 shorter events, 154.8 us)
Async XLA Ops:
  7.2 7.0 copy-start
  7.2 412.3 %all-reduce.7.cloned.1.call-start = ((), (), s32[]{:S(2)}) async-start(), calls=%async_computation.1 | async-start | bytes 2621440 | tf_op jit(solution)/shard_map/psum | solution.py:148
  7.2 7.0 collective-permute-start
  10.8 7.1 collective-permute-start.1
  15.0 16.1 %copy-start.29 = (f32[1,1,2,256,256]{4,3,2,1,0:T(8,128)S(1)}, f32[1,1,2,256,256]{4,3,2,1,0:T(8,128)}, u32[]{:S(2)}) copy-start(f32[1,1,2,256,256]{4,3,2,1,0:T(8,128)} %param.6) | copy-start | bytes 1572868
  17.9 14.2 %copy-start.27 = (f32[2,384,128]{2,1,0:T(8,128)}, f32[2,384,128]{2,1,0:T(8,128)S(1)}, u32[]{:S(2)}) copy-start(f32[2,384,128]{2,1,0:T(8,128)S(1)} %constant_dynamic-update-slice_fusion) | copy-start | bytes 1179652
  18.0 17.0 %collective-permute-start.2 = (f32[2,384,128]{2,1,0:T(8,128)S(1)}, f32[2,384,128]{2,1,0:T(8,128)}, u32[]{:S(2)}, u32[]{:S(2)}) collective-permute-start(f32[2,384,128]{2,1,0:T(8,128)S(1)} %constant_dynamic-update-slice_fusion), channel_id=1, source_target_pairs={{0,1},{1,2},{2,3},{3,4},{4,5},{5,6},{6,7},{7,8},{8,9},{9,10},{10,1... | collective-permute-start | bytes 1179656 | tf_op jit(solution)/shard_map/ppermute | solution.py:24
  19.9 15.1 %collective-permute-start.3 = (f32[2,384,128]{2,1,0:T(8,128)S(1)}, f32[2,384,128]{2,1,0:T(8,128)}, u32[]{:S(2)}, u32[]{:S(2)}) collective-permute-start(f32[2,384,128]{2,1,0:T(8,128)S(1)} %constant_dynamic-update-slice_fusion), channel_id=1, source_target_pairs={{1,0},{2,1},{3,2},{4,3},{5,4},{6,5},{7,6},{8,7},{9,8},{10,9},{11,1... | collective-permute-start | bytes 1179656 | tf_op jit(solution)/shard_map/ppermute | solution.py:26
  122.5 15.2 %collective-permute-start.4 = (f32[3,128,384]{1,2,0:T(8,128)S(1)}, f32[3,128,384]{1,2,0:T(8,128)S(1)}, u32[]{:S(2)}, u32[]{:S(2)}) collective-permute-start(f32[3,128,384]{1,2,0:T(8,128)S(1)} %get-tuple-element.78), channel_id=1, source_target_pairs={{0,16},{16,32},{32,48},{48,64},{64,80},{80,96},{96,112},{112,128},... | collective-permute-start | bytes 1769480 | tf_op jit(solution)/shard_map/ppermute | solution.py:24
  125.3 17.1 %collective-permute-start.5 = (f32[3,128,384]{1,2,0:T(8,128)S(1)}, f32[3,128,384]{1,2,0:T(8,128)S(1)}, u32[]{:S(2)}, u32[]{:S(2)}) collective-permute-start(f32[3,128,384]{1,2,0:T(8,128)S(1)} %get-tuple-element.79), channel_id=1, source_target_pairs={{16,0},{32,16},{48,32},{64,48},{80,64},{96,80},{112,96},{128,112},... | collective-permute-start | bytes 1769480 | tf_op jit(solution)/shard_map/ppermute | solution.py:26
  143.9 277.3 %collective-permute-start.6 = (f32[3,640,128]{1,2,0:T(8,128)}, f32[3,640,128]{1,2,0:T(8,128)}, u32[]{:S(2)}, u32[]{:S(2)}) collective-permute-start(f32[3,640,128]{1,2,0:T(8,128)} %get-tuple-element.70), channel_id=1, source_target_pairs={{0,1},{1,2},{2,3},{3,4},{4,5},{5,6},{6,7},{7,8},{8,9},{9,10},{10,1... | collective-permute-start | bytes 2949128 | tf_op jit(solution)/shard_map/ppermute | solution.py:24
  145.9 275.4 %collective-permute-start.7 = (f32[3,640,128]{1,2,0:T(8,128)}, f32[3,640,128]{1,2,0:T(8,128)}, u32[]{:S(2)}, u32[]{:S(2)}) collective-permute-start(f32[3,640,128]{1,2,0:T(8,128)} %get-tuple-element.71), channel_id=1, source_target_pairs={{1,0},{2,1},{3,2},{4,3},{5,4},{6,5},{7,6},{8,7},{9,8},{10,9},{11,1... | collective-permute-start | bytes 2949128 | tf_op jit(solution)/shard_map/ppermute | solution.py:26
  150.6 660.1 %all-reduce.5.cloned.1.call-start = ((), (), s32[]{:S(2)}) async-start(), calls=%async_computation | async-start | bytes 2621440 | tf_op jit(solution)/shard_map/psum | solution.py:148
  153.5 267.8 %copy-start.24 = (f32[3,128,384]{1,2,0:T(8,128)S(1)}, f32[3,128,384]{1,2,0:T(8,128)}, u32[]{:S(2)}) copy-start(f32[3,128,384]{1,2,0:T(8,128)} %copy-done.23) | copy-start | bytes 1769476
  421.3 6.0 copy-start.26
  421.3 6.0 copy-start.22
  423.0 5.5 collective-permute-start.8
  426.0 6.9 collective-permute-start.9
  432.9 9.1 %collective-permute-start.10 = (f32[2,384,128]{1,2,0:T(8,128)S(1)}, f32[2,384,128]{1,2,0:T(8,128)S(1)}, u32[]{:S(2)}, u32[]{:S(2)}) collective-permute-start(f32[2,384,128]{1,2,0:T(8,128)S(1)} %pad_maximum_fusion.14), channel_id=1, source_target_pairs={{0,1},{1,2},{2,3},{3,4},{4,5},{5,6},{6,7},{7,8},{8,9},{9,10},{10,1... | collective-permute-start | bytes 1179656 | tf_op jit(solution)/shard_map/ppermute | solution.py:24
  434.8 8.9 %collective-permute-start.11 = (f32[2,384,128]{1,2,0:T(8,128)S(1)}, f32[2,384,128]{1,2,0:T(8,128)S(1)}, u32[]{:S(2)}, u32[]{:S(2)}) collective-permute-start(f32[2,384,128]{1,2,0:T(8,128)S(1)} %pad_maximum_fusion.14), channel_id=1, source_target_pairs={{1,0},{2,1},{3,2},{4,3},{5,4},{6,5},{7,6},{8,7},{9,8},{10,9},{11,1... | collective-permute-start | bytes 1179656 | tf_op jit(solution)/shard_map/ppermute | solution.py:26
  523.5 16.1 %collective-permute-start.12 = (f32[3,128,384]{1,2,0:T(8,128)}, f32[3,128,384]{1,2,0:T(8,128)S(1)}, u32[]{:S(2)}, u32[]{:S(2)}) collective-permute-start(f32[3,128,384]{1,2,0:T(8,128)} %get-tuple-element.76), channel_id=1, source_target_pairs={{0,16},{16,32},{32,48},{48,64},{64,80},{80,96},{96,112},{112,128},... | collective-permute-start | bytes 1769480 | tf_op jit(solution)/shard_map/ppermute | solution.py:24
  526.0 17.8 %collective-permute-start.13 = (f32[3,128,384]{1,2,0:T(8,128)}, f32[3,128,384]{1,2,0:T(8,128)}, u32[]{:S(2)}, u32[]{:S(2)}) collective-permute-start(f32[3,128,384]{1,2,0:T(8,128)} %get-tuple-element.77), channel_id=1, source_target_pairs={{16,0},{32,16},{48,32},{64,48},{80,64},{96,80},{112,96},{128,112},... | collective-permute-start | bytes 1769480 | tf_op jit(solution)/shard_map/ppermute | solution.py:26
  546.3 272.8 %collective-permute-start.14 = (f32[3,640,128]{1,2,0:T(8,128)}, f32[3,640,128]{1,2,0:T(8,128)}, u32[]{:S(2)}, u32[]{:S(2)}) collective-permute-start(f32[3,640,128]{1,2,0:T(8,128)} %get-tuple-element.68), channel_id=1, source_target_pairs={{0,1},{1,2},{2,3},{3,4},{4,5},{5,6},{6,7},{7,8},{8,9},{9,10},{10,1... | collective-permute-start | bytes 2949128 | tf_op jit(solution)/shard_map/ppermute | solution.py:24
  548.6 270.5 %collective-permute-start.15 = (f32[3,640,128]{1,2,0:T(8,128)}, f32[3,640,128]{1,2,0:T(8,128)}, u32[]{:S(2)}, u32[]{:S(2)}) collective-permute-start(f32[3,640,128]{1,2,0:T(8,128)} %get-tuple-element.69), channel_id=1, source_target_pairs={{1,0},{2,1},{3,2},{4,3},{5,4},{6,5},{7,6},{8,7},{9,8},{10,9},{11,1... | collective-permute-start | bytes 2949128 | tf_op jit(solution)/shard_map/ppermute | solution.py:26
  (26 other events, 77.3 us)
Sparse Core Ops, SparseCore 0:
  150.7 268.7 all-reduce.6
  531.6 279.0 all-reduce.4
where the time goes:
time: 841 us; the launch traced here: 829 us
  waiting for transfers between devices  563 us (67%)
  local copies, waits for them, and re-layouts  86.8 us (10%)
  matrix products  82 us (10%)
  starting transfers between devices  39.3 us (5%)
  other arithmetic  34.4 us (4%)
  between operations  22.9 us (3%)
    psum x2, waiting for transfers between devices, local(): lax.psum((grad_probe, probe_weight), ('row', 'col'))  525 us
    dynamic_update_slice x4, local copies, waits for them, and re-layouts, local(): lax.dynamic_update_slice(gradient, lax.dynamic_slice(gradient, corner, co...  44.2 us
    dot_general x4, matrix products, last_axis(): jnp.matmul(real_part + imag_part, cos_table + sin_table, precision=HIGHEST)  21.1 us
    ppermute x8, waiting for transfers between devices, padded_2(): lax.ppermute(tail, axis, [(i, (i + 1) % count) for i in range(ends)])  20 us
    ppermute x8, starting transfers between devices, padded_2(): lax.ppermute(tail, axis, [(i, (i + 1) % count) for i in range(ends)])  19.9 us
    ppermute x8, starting transfers between devices, padded_2(): lax.ppermute(head, axis, [((i + 1) % count, i) for i in range(ends)])  19.3 us
    ppermute x8, waiting for transfers between devices, padded_2(): lax.ppermute(head, axis, [((i + 1) % count, i) for i in range(ends)])  17.9 us
  transfers between devices with their start and end apart: 18, of which 11 were waited for; matrix products, arithmetic and copies ran while one was open for 4% of the time, Pallas kernels for 0%

commit v1 on v0

--- a/solution.py
+++ b/solution.py
@@ -145,7 +145,7 @@
             )
         extended = padded_2(gradient, (("row", 1), ("col", 2)), half_width)
         totals = fold_axis(fold_axis(extended, 1, tile_side, half_width), 2, tile_side, half_width)
-        summed_grad, summed_weight = lax.psum((grad_probe, probe_weight), ("row", "col"))
+        summed_grad, summed_weight = lax.psum(lax.psum((grad_probe, probe_weight), "col"), "row")
         new_probe = probe + PROBE_STEP * summed_grad / (summed_weight + PROBE_REG)
         object_field = object_field + OBJECT_STEP * totals[0:2] / (totals[2:3] + OBJECT_REG)
         if iteration + 1 < ITERS:

time: 841 us -> 944 us (1.12)
  waiting for transfers between devices: 563 us -> 680 us
    psum x2 -> x4, waiting for transfers between devices: 525 us -> 636 us  [the longest x2 341 us: local(): lax.psum(lax.psum((grad_probe, probe_weight), 'col'), 'row')]
  transfers between devices with their start and end apart: 18 -> 20, of which waited for: 11 -> 13; matrix products, arithmetic and copies ran while one was open for 4% -> 5% of each run, Pallas kernels for 0% -> 0%
where the time goes in v1:
time: 944 us; the launch traced here: 932 us
  waiting for transfers between devices  680 us (72%)
  local copies, waits for them, and re-layouts  80.4 us (9%)
  matrix products  80.2 us (8%)
  starting transfers between devices  41.7 us (4%)
  other arithmetic  26.1 us (3%)
  between operations  22.9 us (2%)
    psum x2, waiting for transfers between devices, local(): lax.psum(lax.psum((grad_probe, probe_weight), 'col'), 'row')  341 us
    psum x2, waiting for transfers between devices, local(): lax.psum((grad_probe, probe_weight), 'col')  296 us
    dynamic_update_slice x4, local copies, waits for them, and re-layouts, local(): lax.dynamic_update_slice(gradient, lax.dynamic_slice(gradient, corner, co...  44.1 us
    ppermute x8, waiting for transfers between devices, padded_2(): lax.ppermute(tail, axis, [(i, (i + 1) % count) for i in range(ends)])  24.8 us
    ppermute x8, starting transfers between devices, padded_2(): lax.ppermute(tail, axis, [(i, (i + 1) % count) for i in range(ends)])  22.1 us
    dot_general x4, matrix products, last_axis(): jnp.matmul(real_part + imag_part, cos_table + sin_table, precision=HIGHEST)  20.7 us
    ppermute x8, starting transfers between devices, padded_2(): lax.ppermute(head, axis, [((i + 1) % count, i) for i in range(ends)])  19.5 us
  transfers between devices with their start and end apart: 20, of which 13 were waited for; matrix products, arithmetic and copies ran while one was open for 5% of the time, Pallas kernels for 0%

profile of v1, /device:TPU:2, one launch (start us, length us, event | category | flops | bytes accessed | tf_op | source)
XLA Modules:
  0.0 932.0 jit_solution(12314824817777804262)
XLA Ops:
  19.9 3.6 collective-permute-start.3
  36.6 4.0 while.2
  49.6 3.9 fusion.53
  72.7 13.4 %fusion.10 = f32[4,256,256]{2,1,0:T(8,128)S(1)} fusion(f32[4,256,256]{2,1,0:T(8,128)S(1)} %fusion.43, f32[4,256,256]{2,1,0:T(8,128)S(1)} %fusion.62, f32[4,256,256]{1,2,0:T(8,128)S(1)} %get-tuple-element.98, f32[4,256,256]{1,2,0:T(8,128)S(1)} %get-tuple-element.99), kind=kOutput, calls=%fused_computation.34 | convolution fusion | flops 807206912 | bytes 5242880 | tf_op jit(solution)/shard_map/dot_general | solution.py:44
  91.5 4.6 add_reduce_fusion.3
  97.9 10.6 %dynamic_update_slice.12 = f32[3,384,384]{1,2,0:T(8,128)S(1)} dynamic-update-slice(f32[3,384,384]{1,2,0:T(8,128)S(1)} %broadcast.83.clone, f32[3,256,256]{1,2,0:T(8,128)} %pad_maximum_fusion.5, s32[]{:T(128)} %constant.12.clone.1, s32[]{:T(128)S(6)} %select_n.86, s32[]{:T(128)S(6)} %select_n.87) | dynamic-update-slice | bytes 1572868 | tf_op jit(solution)/shard_map/dynamic_update_slice | solution.py:143
  110.7 11.3 %dynamic_update_slice.13 = f32[3,384,384]{1,2,0:T(8,128)S(1)} dynamic-update-slice(f32[3,384,384]{1,2,0:T(8,128)S(1)} %dynamic_update_slice.12, f32[3,256,256]{1,2,0:T(8,128)} %fusion.21, s32[]{:T(128)} %constant.12.clone.1, s32[]{:T(128)S(6)} %select_n.88, s32[]{:T(128)S(6)} %select_n.89) | dynamic-update-slice | bytes 1572868 | tf_op jit(solution)/shard_map/dynamic_update_slice | solution.py:143
  126.2 10.7 %collective-permute-done.4 = f32[3,128,384]{1,2,0:T(8,128)S(1)} collective-permute-done((f32[3,128,384]{1,2,0:T(8,128)S(1)}, f32[3,128,384]{1,2,0:T(8,128)S(1)}, u32[]{:S(2)}, u32[]{:S(2)}) %collective-permute-start.4) | collective-permute-done | bytes 589856 | tf_op jit(solution)/shard_map/ppermute | solution.py:24
  137.0 5.1 collective-permute-done.5
  145.5 3.6 collective-permute-start.7
  152.8 6.5 collective-permute-done.6
  162.6 5.5 collective-permute-start.8
  171.0 4.7 collective-permute-done.9
  182.6 159.7 %all-reduce.11.cloned.1.call-done = (f32[2,2,256,256]{2,3,1,0:T(8,128)}, f32[256,256]{1,0:T(8,128)}) async-done(((f32[2,2,256,256]{2,3,1,0:T(8,128)}, f32[256,256]{1,0:T(8,128)}), (f32[2,2,256,256]{2,3,1,0:T(8,128)}, f32[256,256]{1,0:T(8,128)})) %all-reduce.11.cloned.1.call-update) | async-done | bytes 1310736 | tf_op jit(solution)/shard_map/psum | solution.py:148
  342.6 5.1 while.3
  350.5 167.5 %all-reduce.15.cloned.1.call-done = (f32[2,2,256,256]{2,3,1,0:T(8,128)}, f32[256,256]{1,0:T(8,128)}) async-done(((f32[2,2,256,256]{2,3,1,0:T(8,128)}, f32[256,256]{1,0:T(8,128)}), (f32[2,2,256,256]{2,3,1,0:T(8,128)}, f32[256,256]{1,0:T(8,128)})) %all-reduce.15.cloned.1.call-update) | async-done | bytes 1310736 | tf_op jit(solution)/shard_map/psum | solution.py:148
  525.3 3.9 fusion.50
  565.3 10.9 %dynamic_update_slice.14 = f32[3,384,384]{1,2,0:T(8,128)S(1)} dynamic-update-slice(f32[3,384,384]{1,2,0:T(8,128)S(1)} %broadcast.83, f32[3,256,256]{1,2,0:T(8,128)} %pad_maximum_fusion.7, s32[]{:T(128)} %constant.12.clone.1, s32[]{:T(128)S(6)} %select_n.86, s32[]{:T(128)S(6)} %select_n.87) | dynamic-update-slice | bytes 1572868 | tf_op jit(solution)/shard_map/dynamic_update_slice | solution.py:143
  578.3 11.3 %dynamic_update_slice.15 = f32[3,384,384]{1,2,0:T(8,128)S(1)} dynamic-update-slice(f32[3,384,384]{1,2,0:T(8,128)S(1)} %dynamic_update_slice.14, f32[3,256,256]{1,2,0:T(8,128)} %fusion.20, s32[]{:T(128)} %constant.12.clone.1, s32[]{:T(128)S(6)} %select_n.88, s32[]{:T(128)S(6)} %select_n.89) | dynamic-update-slice | bytes 1572868 | tf_op jit(solution)/shard_map/dynamic_update_slice | solution.py:143
  593.2 6.0 collective-permute-done.12
  599.2 4.4 collective-permute-done.13
  607.1 3.6 collective-permute-start.15
  610.7 135.9 %all-reduce.9.cloned.1.call-done = (f32[2,2,256,256]{2,3,1,0:T(8,128)}, f32[256,256]{1,0:T(8,128)}) async-done(((f32[2,2,256,256]{2,3,1,0:T(8,128)}, f32[256,256]{1,0:T(8,128)}), (f32[2,2,256,256]{2,3,1,0:T(8,128)}, f32[256,256]{1,0:T(8,128)})) %all-reduce.9.cloned.1.call-update) | async-done | bytes 1310736 | tf_op jit(solution)/shard_map/psum | solution.py:148
  749.0 173.3 %all-reduce.13.cloned.1.call-done = (f32[2,2,256,256]{2,3,1,0:T(8,128)}, f32[256,256]{1,0:T(8,128)}) async-done(((f32[2,2,256,256]{2,3,1,0:T(8,128)}, f32[256,256]{1,0:T(8,128)}), (f32[2,2,256,256]{2,3,1,0:T(8,128)}, f32[256,256]{1,0:T(8,128)})) %all-reduce.13.cloned.1.call-update) | async-done | bytes 1310736 | tf_op jit(solution)/shard_map/psum | solution.py:148
  (208 shorter events, 148.3 us)
Async XLA Ops:
  7.2 335.1 %all-reduce.11.cloned.1.call-start = ((), (), s32[]{:S(2)}) async-start(), calls=%async_computation.1 | async-start | bytes 2621440 | tf_op jit(solution)/shard_map/psum | solution.py:148
  7.2 7.0 collective-permute-start
  10.8 7.1 collective-permute-start.1
  18.0 17.2 %collective-permute-start.2 = (f32[2,384,128]{2,1,0:T(8,128)S(1)}, f32[2,384,128]{2,1,0:T(8,128)}, u32[]{:S(2)}, u32[]{:S(2)}) collective-permute-start(f32[2,384,128]{2,1,0:T(8,128)S(1)} %constant_dynamic-update-slice_fusion), channel_id=1, source_target_pairs={{0,1},{1,2},{2,3},{3,4},{4,5},{5,6},{6,7},{7,8},{8,9},{9,10},{10,1... | collective-permute-start | bytes 1179656 | tf_op jit(solution)/shard_map/ppermute | solution.py:24
  19.9 15.3 %collective-permute-start.3 = (f32[2,384,128]{2,1,0:T(8,128)S(1)}, f32[2,384,128]{2,1,0:T(8,128)}, u32[]{:S(2)}, u32[]{:S(2)}) collective-permute-start(f32[2,384,128]{2,1,0:T(8,128)S(1)} %constant_dynamic-update-slice_fusion), channel_id=1, source_target_pairs={{1,0},{2,1},{3,2},{4,3},{5,4},{6,5},{7,6},{8,7},{9,8},{10,9},{11,1... | collective-permute-start | bytes 1179656 | tf_op jit(solution)/shard_map/ppermute | solution.py:26
  122.1 14.9 %collective-permute-start.4 = (f32[3,128,384]{1,2,0:T(8,128)S(1)}, f32[3,128,384]{1,2,0:T(8,128)S(1)}, u32[]{:S(2)}, u32[]{:S(2)}) collective-permute-start(f32[3,128,384]{1,2,0:T(8,128)S(1)} %get-tuple-element.82), channel_id=1, source_target_pairs={{0,16},{16,32},{32,48},{48,64},{64,80},{80,96},{96,112},{112,128},... | collective-permute-start | bytes 1769480 | tf_op jit(solution)/shard_map/ppermute | solution.py:24
  124.6 24.5 %copy-start.12 = (f32[2,256,256]{1,2,0:T(8,128)S(1)}, f32[2,256,256]{1,2,0:T(8,128)}, u32[]{:S(2)}) copy-start(f32[2,256,256]{1,2,0:T(8,128)} %copy.81) | copy-start | bytes 1572868
  124.7 24.5 %copy-start.13 = (f32[2,256,256]{1,2,0:T(8,128)S(1)}, f32[2,256,256]{1,2,0:T(8,128)}, u32[]{:S(2)}) copy-start(f32[2,256,256]{1,2,0:T(8,128)} %copy.84) | copy-start | bytes 1572868
  124.7 24.5 %copy-start.23 = (f32[4,256,256]{1,2,0:T(8,128)S(1)}, f32[4,256,256]{1,2,0:T(8,128)}, u32[]{:S(2)}) copy-start(f32[4,256,256]{1,2,0:T(8,128)} %get-tuple-element.65) | copy-start | bytes 3145732
  124.7 17.4 %collective-permute-start.5 = (f32[3,128,384]{1,2,0:T(8,128)S(1)}, f32[3,128,384]{1,2,0:T(8,128)S(1)}, u32[]{:S(2)}, u32[]{:S(2)}) collective-permute-start(f32[3,128,384]{1,2,0:T(8,128)S(1)} %get-tuple-element.83), channel_id=1, source_target_pairs={{16,0},{32,16},{48,32},{64,48},{80,64},{96,80},{112,96},{128,112},... | collective-permute-start | bytes 1769480 | tf_op jit(solution)/shard_map/ppermute | solution.py:26
  143.5 15.7 %collective-permute-start.6 = (f32[3,640,128]{1,2,0:T(8,128)}, f32[3,640,128]{1,2,0:T(8,128)}, u32[]{:S(2)}, u32[]{:S(2)}) collective-permute-start(f32[3,640,128]{1,2,0:T(8,128)} %get-tuple-element.74), channel_id=1, source_target_pairs={{0,1},{1,2},{2,3},{3,4},{4,5},{5,6},{6,7},{7,8},{8,9},{9,10},{10,1... | collective-permute-start | bytes 2949128 | tf_op jit(solution)/shard_map/ppermute | solution.py:24
  145.5 15.6 %collective-permute-start.7 = (f32[3,640,128]{1,2,0:T(8,128)}, f32[3,640,128]{1,2,0:T(8,128)}, u32[]{:S(2)}, u32[]{:S(2)}) collective-permute-start(f32[3,640,128]{1,2,0:T(8,128)} %get-tuple-element.75), channel_id=1, source_target_pairs={{1,0},{2,1},{3,2},{4,3},{5,4},{6,5},{7,6},{8,7},{9,8},{10,9},{11,1... | collective-permute-start | bytes 2949128 | tf_op jit(solution)/shard_map/ppermute | solution.py:26
  151.9 366.2 %all-reduce.15.cloned.1.call-start = ((), (), s32[]{:S(2)}) async-start(), calls=%async_computation.3 | async-start | bytes 2621440 | tf_op jit(solution)/shard_map/psum | solution.py:148
  162.6 8.4 collective-permute-start.8
  168.2 7.5 collective-permute-start.9
  175.7 166.7 %collective-permute-start.10 = (f32[2,384,128]{1,2,0:T(8,128)S(1)}, f32[2,384,128]{1,2,0:T(8,128)S(1)}, u32[]{:S(2)}, u32[]{:S(2)}) collective-permute-start(f32[2,384,128]{1,2,0:T(8,128)S(1)} %pad_maximum_fusion.14), channel_id=1, source_target_pairs={{0,1},{1,2},{2,3},{3,4},{4,5},{5,6},{6,7},{7,8},{8,9},{9,10},{10,1... | collective-permute-start | bytes 1179656 | tf_op jit(solution)/shard_map/ppermute | solution.py:24
  178.2 164.2 %collective-permute-start.11 = (f32[2,384,128]{1,2,0:T(8,128)S(1)}, f32[2,384,128]{1,2,0:T(8,128)S(1)}, u32[]{:S(2)}, u32[]{:S(2)}) collective-permute-start(f32[2,384,128]{1,2,0:T(8,128)S(1)} %pad_maximum_fusion.14), channel_id=1, source_target_pairs={{1,0},{2,1},{3,2},{4,3},{5,4},{6,5},{7,6},{8,7},{9,8},{10,9},{11,1... | collective-permute-start | bytes 1179656 | tf_op jit(solution)/shard_map/ppermute | solution.py:26
  342.3 404.3 %all-reduce.9.cloned.1.call-start = ((), (), s32[]{:S(2)}) async-start(), calls=%async_computation | async-start | bytes 2621440 | tf_op jit(solution)/shard_map/psum | solution.py:148
  349.8 170.2 %copy-start.22 = (f32[2,2,256,256]{2,3,1,0:T(8,128)S(1)}, f32[2,2,256,256]{2,3,1,0:T(8,128)}, u32[]{:S(2)}) copy-start(f32[2,2,256,256]{2,3,1,0:T(8,128)} %copy.102) | copy-start | bytes 3145732
  564.2 358.1 %all-reduce.13.cloned.1.call-start = ((), (), s32[]{:S(2)}) async-start(), calls=%async_computation.2 | async-start | bytes 2621440 | tf_op jit(solution)/shard_map/psum | solution.py:148
  589.7 9.5 %collective-permute-start.12 = (f32[3,128,384]{1,2,0:T(8,128)S(1)}, f32[3,128,384]{1,2,0:T(8,128)S(1)}, u32[]{:S(2)}, u32[]{:S(2)}) collective-permute-start(f32[3,128,384]{1,2,0:T(8,128)S(1)} %get-tuple-element.80), channel_id=1, source_target_pairs={{0,16},{16,32},{32,48},{48,64},{64,80},{80,96},{96,112},{112,128},... | collective-permute-start | bytes 1769480 | tf_op jit(solution)/shard_map/ppermute | solution.py:24
  591.9 11.8 %collective-permute-start.13 = (f32[3,128,384]{1,2,0:T(8,128)S(1)}, f32[3,128,384]{1,2,0:T(8,128)S(1)}, u32[]{:S(2)}, u32[]{:S(2)}) collective-permute-start(f32[3,128,384]{1,2,0:T(8,128)S(1)} %get-tuple-element.81), channel_id=1, source_target_pairs={{16,0},{32,16},{48,32},{64,48},{80,64},{96,80},{112,96},{128,112},... | collective-permute-start | bytes 1769480 | tf_op jit(solution)/shard_map/ppermute | solution.py:26
  605.1 141.5 %collective-permute-start.14 = (f32[3,640,128]{1,2,0:T(8,128)}, f32[3,640,128]{1,2,0:T(8,128)}, u32[]{:S(2)}, u32[]{:S(2)}) collective-permute-start(f32[3,640,128]{1,2,0:T(8,128)} %get-tuple-element.72), channel_id=1, source_target_pairs={{0,1},{1,2},{2,3},{3,4},{4,5},{5,6},{6,7},{7,8},{8,9},{9,10},{10,1... | collective-permute-start | bytes 2949128 | tf_op jit(solution)/shard_map/ppermute | solution.py:24
  607.1 139.6 %collective-permute-start.15 = (f32[3,640,128]{1,2,0:T(8,128)}, f32[3,640,128]{1,2,0:T(8,128)}, u32[]{:S(2)}, u32[]{:S(2)}) collective-permute-start(f32[3,640,128]{1,2,0:T(8,128)} %get-tuple-element.73), channel_id=1, source_target_pairs={{1,0},{2,1},{3,2},{4,3},{5,4},{6,5},{7,6},{8,7},{9,8},{10,9},{11,1... | collective-permute-start | bytes 2949128 | tf_op jit(solution)/shard_map/ppermute | solution.py:26
  (30 other events, 120.0 us)
Sparse Core Ops, SparseCore 0:
  152.0 190.2 all-reduce.10
  345.0 173.0 all-reduce.14
  564.3 182.2 all-reduce.8
  749.2 173.0 all-reduce.12
